TPU v7x, 512 devices: a whole 4x4x16 slice. The times are simulated.
512 devices in a mesh: walk: 64 (over z, y), col: 8 (over x, core).
Axes of the slice: x: 4, y: 4, z: 16, core: 2. Of those that a mesh axis runs over, the one named last changes fastest.
Arguments:
- jacobian: float32 [384, 524288], P('walk', 'col'), may hold values from -25 to 25
- prev_update: float32 [8, 65536], P('col', 'walk'), may hold values from -6 to 6
- base_energy: float32 [384], P('walk'), may hold values from -6 to 6
- elec_pos: float32 [384, 3, 66], P('walk'), may hold values from -8 to 8
- atom_pos: float32 [3, 21], replicated, may hold values from -6 to 6
- quad_ratio: float32 [384, 21, 66, 12], P('walk'), may hold values from -1.2 to 1.2
- rotation: int32 [384, 66], P('walk'), may hold values from 0 to 15
- channels: int32 [21], replicated, may hold values from 1 to 3
- ecp_coef: float32 [21, 3], replicated, may hold values from 0.5 to 2
- ecp_expo: float32 [21, 3], replicated, may hold values from 0.2 to 2
Outputs:
- local_energy: float32 [384], P('walk')
- update: float32 [8, 65536], P('col', 'walk')
All inputs are finite; a program needn't handle non-finite values.
Results may differ from a plain program's by a relative error of at most 0.0003.
Values sent between devices are 32-bit elements; how exact they have to be, the bound alone decides.
No kernel may reach another device: no remote copies, remote signals or barrier semaphores. Data moves between devices by JAX's collectives and lax.ppermute only.
A program may use at most 64 MiB of HBM per device.

v0:
```python
import math
import jax
import jax.numpy as jnp
from jax import lax
from jax.sharding import PartitionSpec as P

NROT = 16
momentum = 0.9
damping = 0.1


def icosa_points():
    golden = (1.0 + math.sqrt(5.0)) / 2.0
    length = math.sqrt(1.0 + golden * golden)
    rows = []
    for first in (-1.0, 1.0):
        for second in (-golden, golden):
            rows.append((0.0, first / length, second / length))
            rows.append((first / length, second / length, 0.0))
            rows.append((second / length, 0.0, first / length))
    return jnp.asarray(rows, dtype=jnp.float32).T


def rotation_table(count):
    angle = jnp.arange(count, dtype=jnp.float32)
    turn_z = 2.0 * math.pi * angle / count
    turn_x = 0.9 * angle
    cz, sz = (jnp.cos(turn_z), jnp.sin(turn_z))
    cx, sx = (jnp.cos(turn_x), jnp.sin(turn_x))
    zeros = jnp.zeros_like(cz)
    matrix = jnp.stack(
        [
            jnp.stack([cz, -sz * cx, sz * sx], axis=-1),
            jnp.stack([sz, cz * cx, -cz * sx], axis=-1),
            jnp.stack([zeros, sx, cx], axis=-1),
        ],
        axis=1,
    )
    points = icosa_points()
    rotated = matrix[:, :, 0, None] * points[None, 0, :]
    rotated = rotated + matrix[:, :, 1, None] * points[None, 1, :]
    rotated = rotated + matrix[:, :, 2, None] * points[None, 2, :]
    return rotated.reshape(count, -1)


def nonlocal_energy(elec_pos, atom_pos, quad_ratio, rotation, channels, ecp_coef, ecp_expo):
    walkers, electrons = rotation.shape
    count = NROT
    table = rotation_table(count)
    onehot = (rotation[:, :, None] == jnp.arange(count, dtype=jnp.int32)[None, None, :]).astype(
        jnp.float32
    )
    rotated = jnp.einsum("wek,kf->wef", onehot, table, precision=lax.Precision.HIGHEST)
    rotated = rotated.reshape(walkers, electrons, 3, -1)
    diff = elec_pos[:, :, None, :] - atom_pos[None, :, :, None]
    dist2 = jnp.sum(diff * diff, axis=1)
    unit = diff / jnp.sqrt(dist2 + 0.01)[:, None, :, :]
    cosang = unit[:, 0, :, :, None] * rotated[:, None, :, 0, :]
    cosang = cosang + unit[:, 1, :, :, None] * rotated[:, None, :, 1, :]
    cosang = cosang + unit[:, 2, :, :, None] * rotated[:, None, :, 2, :]
    quad = quad_ratio.shape[-1]
    lmax = ecp_coef.shape[1]
    lower = jnp.ones_like(cosang)
    upper = cosang
    total = jnp.zeros((walkers,), jnp.float32)
    for level in range(lmax):
        if level == 0:
            poly = lower
        elif level == 1:
            poly = upper
        else:
            fresh = ((2 * level - 1) * cosang * upper - (level - 1) * lower) / level
            lower, upper = (upper, fresh)
            poly = fresh
        angular = jnp.sum(poly * quad_ratio, axis=-1) / quad
        active = (channels > level).astype(jnp.float32)
        radial = ecp_coef[None, :, level, None] * jnp.exp(-ecp_expo[None, :, level, None] * dist2)
        term = (2 * level + 1) * active[None, :, None] * radial * angular
        total = total + jnp.sum(term, axis=(1, 2))
    return total


def sum_pieces(first, second):
    first_sum, second_sum = lax.psum((first, second), ("walk", "col"))
    return (first_sum, second_sum)


def body(
    jacobian,
    prev_update,
    base_energy,
    elec_pos,
    atom_pos,
    quad_ratio,
    rotation,
    channels,
    ecp_coef,
    ecp_expo,
):
    energy_mine = base_energy + nonlocal_energy(
        elec_pos, atom_pos, quad_ratio, rotation, channels, ecp_coef, ecp_expo
    )
    columns = lax.all_to_all(jacobian, "walk", split_axis=1, concat_axis=0, tiled=True)
    walkers = columns.shape[0]
    params_total = columns.shape[1] * lax.axis_size("walk") * lax.axis_size("col")
    scale = 1.0 / params_total
    centred = columns - jnp.mean(columns, axis=0, keepdims=True)
    prev_mine = prev_update[0]
    gram_part = (
        jnp.dot(
            centred, centred.T, precision=lax.Precision.HIGHEST, preferred_element_type=jnp.float32
        )
        * scale
    )
    along_part = (
        jnp.dot(
            centred, prev_mine, precision=lax.Precision.HIGHEST, preferred_element_type=jnp.float32
        )
        * scale
    )
    extra = along_part[:, None]
    gram, extra_sum = sum_pieces(gram_part, extra)
    along = extra_sum[:, 0]
    energies = lax.all_gather(energy_mine, "walk", axis=0, tiled=True)
    eps = -(energies - jnp.mean(energies)) / math.sqrt(walkers)
    system = gram + damping * jnp.eye(walkers, dtype=jnp.float32)
    factor = jnp.linalg.cholesky(system)
    solved = jax.scipy.linalg.cho_solve((factor, True), eps - momentum * along)
    update_mine = (
        jnp.dot(
            solved, centred, precision=lax.Precision.HIGHEST, preferred_element_type=jnp.float32
        )
        + momentum * prev_mine
    )
    return (energy_mine, update_mine[None, :])


def solution(mesh):
    in_specs = (
        P("walk", "col"),
        P("col", "walk"),
        P("walk"),
        P("walk", None, None),
        P(),
        P("walk", None, None, None),
        P("walk", None),
        P(),
        P(),
        P(),
    )
    out_specs = (P("walk"), P("col", "walk"))
    return jax.shard_map(body, mesh=mesh, in_specs=in_specs, out_specs=out_specs, check_vma=False)
```

profile of v0, /device:TPU:1, one launch (start us, length us, event | category | flops | bytes accessed | tf_op | source)
XLA Modules:
  0.0 826.4 jit_solution(6028116304954348564)
XLA Ops:
  7.3 19.4 %all-to-all-start = ((f32[6,64,1024]{2,0,1:T(8,128)}), f32[6,64,1024]{2,0,1:T(8,128)S(1)}, u32[]{:S(2)}, u32[]{:S(2)}) async-start(f32[6,64,1024]{2,0,1:T(8,128)} %bitcast.162), calls=%async_computation | async-start | bytes 4194304 | tf_op jit(solution)/shard_map/all_to_all | solution.py:103
  28.4 1.3 dynamic-slice.3
  32.3 187.9 %all-reduce.1 = f32[384]{0:T(512)S(1)} all-reduce(f32[384]{0:T(512)S(1)} %get-tuple-element.32), channel_id=1, replica_groups=mesh['walk'=64,'col'=8] {'walk'}, use_global_device_ids=true, to_apply=%add.1 | all-reduce | flops 384 | bytes 3072
  221.7 1.6 subtract_bitcast_fusion
  223.3 1.6 sub.49
  225.0 3.4 convolution_multiply_fusion
  228.4 1.4 convolution_reduce_fusion
  229.9 133.3 %psum.15 = f32[384,1]{0,1:T(1,128)S(1)} all-reduce(f32[384,1]{0,1:T(1,128)S(1)} %broadcast_in_dim.6), channel_id=1, replica_groups=mesh['walk'=64,'col'=8] {'walk','col'}, use_global_device_ids=true, to_apply=%region_16.17 | all-reduce | flops 384 | bytes 3072 | tf_op jit(solution)/shard_map/psum | solution.py:84
  363.3 355.0 %all-reduce.4.cloned.1.call-done = f32[384,384]{0,1:T(8,128)} async-done(((f32[384,384]{0,1:T(8,128)}), f32[384,384]{0,1:T(8,128)}) %all-reduce.4.cloned.1.call-update) | async-done | bytes 589840 | tf_op jit(solution)/shard_map/psum | solution.py:84
  718.2 1.2 select_add_fusion
  719.8 11.7 %cholesky.76 = f32[128,128]{1,0:T(8,128)S(1)} custom-call(f32[128,128]{1,0:T(8,128)S(1)} %cholesky.189), custom_call_target="Cholesky" | custom-call | tf_op jit(solution)/shard_map/jit(cholesky)/cholesky | solution.py:127
  731.5 9.8 %custom-call.26 = f32[1,128,128]{1,2,0:T(8,128)S(1)} custom-call(f32[1,128,128]{2,1,0:T(8,128)S(1)} %get-tuple-element.45), custom_call_target="InvertDiagBlocksLowerTriangular" | custom-call | tf_op jit(solution)/shard_map/jit(cholesky)/cholesky | solution.py:127
  742.1 11.7 %cholesky.160 = f32[128,128]{1,0:T(8,128)S(1)} custom-call(f32[128,128]{1,0:T(8,128)S(1)} %cholesky.193), custom_call_target="Cholesky" | custom-call | tf_op jit(solution)/shard_map/jit(cholesky)/cholesky | solution.py:127
  754.0 10.0 %custom-call.27 = f32[1,128,128]{1,2,0:T(8,128)S(1)} custom-call(f32[1,128,128]{2,1,0:T(8,128)S(1)} %get-tuple-element.43), custom_call_target="InvertDiagBlocksLowerTriangular" | custom-call | tf_op jit(solution)/shard_map/jit(cholesky)/cholesky | solution.py:127
  764.7 11.7 %cholesky.179 = f32[128,128]{1,0:T(8,128)S(1)} custom-call(f32[128,128]{1,0:T(8,128)S(1)} %convolution_subtract_fusion.1), custom_call_target="Cholesky" | custom-call | tf_op jit(solution)/shard_map/jit(cholesky)/cholesky | solution.py:127
  776.6 0.7 compare_reduce_fusion
  777.3 0.6 compare_reduce_fusion.1
  779.9 6.7 while.1
  780.6 1.4 dynamic-slice.8
  782.8 1.4 dynamic-slice.8
  785.0 1.4 dynamic-slice.8
  786.6 29.5 %custom-call.28 = f32[3,128,128]{1,2,0:T(8,128)S(1)} custom-call(f32[3,128,128]{2,1,0:T(8,128)S(1)} %get-tuple-element.9), custom_call_target="InvertDiagBlocksLowerTriangular" | custom-call | tf_op jit(solution)/shard_map/jit(_cho_solve)/triangular_solve | solution.py:128
  818.0 0.9 fusion.33
  818.9 0.6 multiply_add_fusion.1
  (123 shorter events, 10.7 us)
Async XLA Ops:
  7.2 20.8 %copy-start.11 = (f32[12]{0:T(128)S(1)}, f32[12]{0:T(128)}, u32[]{:S(2)}) copy-start(f32[12]{0:T(128)} %constant.198) | copy-start | bytes 148
  7.2 20.9 %copy-start.10 = (f32[12]{0:T(128)S(1)}, f32[12]{0:T(128)}, u32[]{:S(2)}) copy-start(f32[12]{0:T(128)} %constant.200) | copy-start | bytes 148
  7.2 20.9 %copy-start.9 = (f32[12]{0:T(128)S(1)}, f32[12]{0:T(128)}, u32[]{:S(2)}) copy-start(f32[12]{0:T(128)} %constant.202) | copy-start | bytes 148
  7.2 21.2 %copy-start.3 = (f32[6,3,66]{2,1,0:T(4,128)S(1)}, f32[6,3,66]{2,1,0:T(4,128)}, u32[]{:S(2)}) copy-start(f32[6,3,66]{2,1,0:T(4,128)} %param.14) | copy-start | bytes 14260
  7.2 23.1 %copy-start.4 = (f32[3,21]{1,0:T(4,128)S(1)}, f32[3,21]{1,0:T(4,128)}, u32[]{:S(2)}) copy-start(f32[3,21]{1,0:T(4,128)} %param.15) | copy-start | bytes 760
  7.2 23.2 %copy-start.12 = (s32[21]{0:T(128)S(1)}, s32[21]{0:T(128)}, u32[]{:S(2)}) copy-start(s32[21]{0:T(128)} %param.18) | copy-start | bytes 256
  7.2 23.3 %copy-start.6 = (f32[21,3]{0,1:T(4,128)S(1)}, f32[21,3]{0,1:T(4,128)}, u32[]{:S(2)}) copy-start(f32[21,3]{0,1:T(4,128)} %param.20) | copy-start | bytes 760
  7.2 23.3 %copy-start.7 = (f32[21,3]{0,1:T(4,128)S(1)}, f32[21,3]{0,1:T(4,128)}, u32[]{:S(2)}) copy-start(f32[21,3]{0,1:T(4,128)} %param.19) | copy-start | bytes 760
  7.3 23.3 %copy-start.5 = (s32[6,66]{1,0:T(8,128)S(1)}, s32[6,66]{1,0:T(8,128)}, u32[]{:S(2)}) copy-start(s32[6,66]{1,0:T(8,128)} %param.17) | copy-start | bytes 4756
  7.3 214.3 %all-to-all-start = ((f32[6,64,1024]{2,0,1:T(8,128)}), f32[6,64,1024]{2,0,1:T(8,128)S(1)}, u32[]{:S(2)}, u32[]{:S(2)}) async-start(f32[6,64,1024]{2,0,1:T(8,128)} %bitcast.162), calls=%async_computation | async-start | bytes 4194304 | tf_op jit(solution)/shard_map/all_to_all | solution.py:103
  26.7 4.2 copy-start.1
  26.7 691.5 %all-reduce.4.cloned.1.call-start = ((), (), s32[]{:S(2)}) async-start(), calls=%async_computation.1 | async-start | bytes 1179648 | tf_op jit(solution)/shard_map/psum | solution.py:84
  30.5 1.2 copy-start.8
  225.0 3.5 copy-start.2
  718.2 1.4 copy-start
Sparse Core Ops, SparseCore 0:
  228.5 489.6 all-reduce.3
where the time goes:
time: 827 us; the launch traced here: 826 us
  waiting for transfers between devices  355 us (43%)
  blocking collectives  321 us (39%)
  other arithmetic  92.2 us (11%)
  starting transfers between devices  19.5 us (2%)
  between operations  17.8 us (2%)
  local copies, waits for them, and re-layouts  11.5 us (1%)
  matrix products  9.1 us (1%)
    psum x1, waiting for transfers between devices, sum_pieces(): first_sum, second_sum = lax.psum((first, second), ('walk', 'col'))  355 us
    unnamed x1, blocking collectives  188 us
    psum x1, blocking collectives, sum_pieces(): first_sum, second_sum = lax.psum((first, second), ('walk', 'col'))  133 us
    another operation x10, other arithmetic, body(): factor = jnp.linalg.cholesky(system)  56.4 us
    another operation x3, other arithmetic, body(): solved = jax.scipy.linalg.cho_solve((factor, True), eps - momentum * along)  29.5 us
    all_to_all x1, starting transfers between devices, body(): lax.all_to_all(jacobian, 'walk', split_axis=1, concat_axis=0, tiled=True)  19.4 us
  transfers between devices with their start and end apart: 2, of which 1 were waited for; matrix products, arithmetic and copies ran while one was open for 1% of the time, Pallas kernels for 0%

commit v1 on v0

--- a/solution.py
+++ b/solution.py
@@ -100,7 +100,10 @@
     energy_mine = base_energy + nonlocal_energy(
         elec_pos, atom_pos, quad_ratio, rotation, channels, ecp_coef, ecp_expo
     )
-    columns = lax.all_to_all(jacobian, "walk", split_axis=1, concat_axis=0, tiled=True)
+    columns = jnp.concatenate(
+        lax.all_to_all(jnp.stack(jnp.split(jacobian, lax.axis_size("walk"), axis=1)), "walk", 0, 0),
+        axis=0,
+    )
     walkers = columns.shape[0]
     params_total = columns.shape[1] * lax.axis_size("walk") * lax.axis_size("col")
     scale = 1.0 / params_total

time: 827 us -> 918 us (1.11)
  local copies, waits for them, and re-layouts: 11.5 us -> 98.6 us
    unnamed x29 -> x92, local copies, waits for them, and re-layouts: 1.34 us -> 87.1 us
where the time goes in v1:
time: 918 us; the launch traced here: 914 us
  waiting for transfers between devices  355 us (39%)
  blocking collectives  321 us (35%)
  local copies, waits for them, and re-layouts  98.6 us (11%)
  other arithmetic  92.2 us (10%)
  starting transfers between devices  19.5 us (2%)
  between operations  17.8 us (2%)
    psum x1, waiting for transfers between devices, sum_pieces(): first_sum, second_sum = lax.psum((first, second), ('walk', 'col'))  355 us
    unnamed x1, blocking collectives  188 us
    psum x1, blocking collectives, sum_pieces(): first_sum, second_sum = lax.psum((first, second), ('walk', 'col'))  133 us
    unnamed x92, local copies, waits for them, and re-layouts  87.1 us
    another operation x10, other arithmetic, body(): factor = jnp.linalg.cholesky(system)  56.4 us
    another operation x3, other arithmetic, body(): solved = jax.scipy.linalg.cho_solve((factor, True), eps - momentum * along)  29.5 us
    all_to_all x1, starting transfers between devices, body(): lax.all_to_all(jnp.stack(jnp.split(jacobian, lax.axis_size('walk'), axis=...  19.4 us
  transfers between devices with their start and end apart: 2, of which 1 were waited for; matrix products, arithmetic and copies ran while one was open for 1% of the time, Pallas kernels for 0%

profile of v1, /device:TPU:1, one launch (start us, length us, event | category | flops | bytes accessed | tf_op | source)
XLA Modules:
  0.0 913.6 jit_solution(14875431696284601700)
XLA Ops:
  14.0 1.4 constant_dynamic-update-slice_fusion.58
  20.8 1.4 constant_dynamic-update-slice_fusion.53
  48.0 1.4 constant_dynamic-update-slice_fusion.33
  57.6 1.4 constant_dynamic-update-slice_fusion.26
  60.3 1.4 constant_dynamic-update-slice_fusion.24
  68.5 1.4 constant_dynamic-update-slice_fusion.18
  94.4 19.4 %all-to-all-start = ((f32[64,6,1024]{2,1,0:T(8,128)}), f32[64,6,1024]{2,1,0:T(8,128)S(1)}, u32[]{:S(2)}, u32[]{:S(2)}) async-start(f32[64,6,1024]{2,1,0:T(8,128)} %constant_dynamic-update-slice_fusion), calls=%async_computation | async-start | bytes 4194304 | tf_op jit(solution)/shard_map/all_to_all | solution.py:104
  119.5 188.0 %all-reduce.1 = f32[384]{0:T(512)S(1)} all-reduce(f32[384]{0:T(512)S(1)} %get-tuple-element.32), channel_id=1, replica_groups=mesh['walk'=64,'col'=8] {'walk'}, use_global_device_ids=true, to_apply=%add.1 | all-reduce | flops 384 | bytes 3072
  308.9 1.6 broadcast_subtract_fusion
  310.5 1.6 sub.45
  312.1 3.4 convolution_multiply_fusion
  315.6 1.4 convolution_reduce_fusion
  317.1 133.2 %psum.15 = f32[384,1]{0,1:T(1,128)S(1)} all-reduce(f32[384,1]{0,1:T(1,128)S(1)} %broadcast_in_dim.6), channel_id=1, replica_groups=mesh['walk'=64,'col'=8] {'walk','col'}, use_global_device_ids=true, to_apply=%region_16.17 | all-reduce | flops 384 | bytes 3072 | tf_op jit(solution)/shard_map/psum | solution.py:84
  450.3 355.2 %all-reduce.4.cloned.1.call-done = f32[384,384]{0,1:T(8,128)} async-done(((f32[384,384]{0,1:T(8,128)}), f32[384,384]{0,1:T(8,128)}) %all-reduce.4.cloned.1.call-update) | async-done | bytes 589840 | tf_op jit(solution)/shard_map/psum | solution.py:84
  807.0 11.7 %cholesky.76 = f32[128,128]{1,0:T(8,128)S(1)} custom-call(f32[128,128]{1,0:T(8,128)S(1)} %cholesky.189), custom_call_target="Cholesky" | custom-call | tf_op jit(solution)/shard_map/jit(cholesky)/cholesky | solution.py:130
  818.8 9.8 %custom-call.26 = f32[1,128,128]{1,2,0:T(8,128)S(1)} custom-call(f32[1,128,128]{2,1,0:T(8,128)S(1)} %get-tuple-element.45), custom_call_target="InvertDiagBlocksLowerTriangular" | custom-call | tf_op jit(solution)/shard_map/jit(cholesky)/cholesky | solution.py:130
  829.3 11.7 %cholesky.160 = f32[128,128]{1,0:T(8,128)S(1)} custom-call(f32[128,128]{1,0:T(8,128)S(1)} %cholesky.193), custom_call_target="Cholesky" | custom-call | tf_op jit(solution)/shard_map/jit(cholesky)/cholesky | solution.py:130
  841.2 10.0 %custom-call.27 = f32[1,128,128]{1,2,0:T(8,128)S(1)} custom-call(f32[1,128,128]{2,1,0:T(8,128)S(1)} %get-tuple-element.43), custom_call_target="InvertDiagBlocksLowerTriangular" | custom-call | tf_op jit(solution)/shard_map/jit(cholesky)/cholesky | solution.py:130
  852.0 11.7 %cholesky.179 = f32[128,128]{1,0:T(8,128)S(1)} custom-call(f32[128,128]{1,0:T(8,128)S(1)} %convolution_subtract_fusion.1), custom_call_target="Cholesky" | custom-call | tf_op jit(solution)/shard_map/jit(cholesky)/cholesky | solution.py:130
  867.1 6.7 while.1
  867.8 1.4 dynamic-slice.8
  870.1 1.4 dynamic-slice.8
  872.3 1.4 dynamic-slice.8
  873.9 29.5 %custom-call.28 = f32[3,128,128]{1,2,0:T(8,128)S(1)} custom-call(f32[3,128,128]{2,1,0:T(8,128)S(1)} %get-tuple-element.9), custom_call_target="InvertDiagBlocksLowerTriangular" | custom-call | tf_op jit(solution)/shard_map/jit(_cho_solve)/triangular_solve | solution.py:131
  (187 shorter events, 95.0 us)
Async XLA Ops:
  94.4 20.8 %copy-start.11 = (f32[12]{0:T(128)S(1)}, f32[12]{0:T(128)}, u32[]{:S(2)}) copy-start(f32[12]{0:T(128)} %constant.198) | copy-start | bytes 148
  94.4 20.8 %copy-start.10 = (f32[12]{0:T(128)S(1)}, f32[12]{0:T(128)}, u32[]{:S(2)}) copy-start(f32[12]{0:T(128)} %constant.200) | copy-start | bytes 148
  94.4 20.9 %copy-start.9 = (f32[12]{0:T(128)S(1)}, f32[12]{0:T(128)}, u32[]{:S(2)}) copy-start(f32[12]{0:T(128)} %constant.202) | copy-start | bytes 148
  94.4 21.2 %copy-start.3 = (f32[6,3,66]{2,1,0:T(4,128)S(1)}, f32[6,3,66]{2,1,0:T(4,128)}, u32[]{:S(2)}) copy-start(f32[6,3,66]{2,1,0:T(4,128)} %param.14) | copy-start | bytes 14260
  94.4 23.2 %copy-start.4 = (f32[3,21]{1,0:T(4,128)S(1)}, f32[3,21]{1,0:T(4,128)}, u32[]{:S(2)}) copy-start(f32[3,21]{1,0:T(4,128)} %param.15) | copy-start | bytes 760
  94.4 23.3 %copy-start.12 = (s32[21]{0:T(128)S(1)}, s32[21]{0:T(128)}, u32[]{:S(2)}) copy-start(s32[21]{0:T(128)} %param.18) | copy-start | bytes 256
  94.4 23.3 %copy-start.6 = (f32[21,3]{0,1:T(4,128)S(1)}, f32[21,3]{0,1:T(4,128)}, u32[]{:S(2)}) copy-start(f32[21,3]{0,1:T(4,128)} %param.20) | copy-start | bytes 760
  94.4 23.3 %copy-start.7 = (f32[21,3]{0,1:T(4,128)S(1)}, f32[21,3]{0,1:T(4,128)}, u32[]{:S(2)}) copy-start(f32[21,3]{0,1:T(4,128)} %param.19) | copy-start | bytes 760
  94.4 23.3 %copy-start.5 = (s32[6,66]{1,0:T(8,128)S(1)}, s32[6,66]{1,0:T(8,128)}, u32[]{:S(2)}) copy-start(s32[6,66]{1,0:T(8,128)} %param.17) | copy-start | bytes 4756
  94.4 23.7 %copy-start.1 = (f32[6,21,66,12]{2,1,3,0:T(8,128)S(1)}, f32[6,21,66,12]{2,1,3,0:T(8,128)}, u32[]{:S(2)}) copy-start(f32[6,21,66,12]{2,1,3,0:T(8,128)} %param.16) | copy-start | bytes 1197508
  94.4 214.3 %all-to-all-start = ((f32[64,6,1024]{2,1,0:T(8,128)}), f32[64,6,1024]{2,1,0:T(8,128)S(1)}, u32[]{:S(2)}, u32[]{:S(2)}) async-start(f32[64,6,1024]{2,1,0:T(8,128)} %constant_dynamic-update-slice_fusion), calls=%async_computation | async-start | bytes 4194304 | tf_op jit(solution)/shard_map/all_to_all | solution.py:104
  113.9 5.1 copy-start.8
  113.9 691.6 %all-reduce.4.cloned.1.call-start = ((), (), s32[]{:S(2)}) async-start(), calls=%async_computation.1 | async-start | bytes 1179648 | tf_op jit(solution)/shard_map/psum | solution.py:84
  312.1 3.5 copy-start.2
  805.5 1.4 copy-start
Sparse Core Ops, SparseCore 0:
  315.7 489.7 all-reduce.3
